TPU v7x, 32 devices: a whole 2x2x4 slice. The times are simulated.
32 devices in a mesh: ctx: 4 (over z), exp: 8 (over y, x, core).
Axes of the slice: x: 2, y: 2, z: 4, core: 2. Of those that a mesh axis runs over, the one named last changes fastest.
Arguments:
- hidden_in: bfloat16 [4096, 2880], P(('ctx', 'exp')), may hold values from -6 to 6
- query_rows: bfloat16 [4096, 2048], P(('ctx', 'exp')), may hold values from -6 to 6
- key_rows: bfloat16 [4096, 256], P(('ctx', 'exp')), may hold values from -6 to 6
- value_rows: bfloat16 [4096, 256], P(('ctx', 'exp')), may hold values from -6 to 6
- sink_logits: float32 [32], replicated, may hold values from -1 to 3
- out_weight: bfloat16 [2048, 2880], replicated, may hold values from -0.125 to 0.125
- norm_gain: float32 [2880], replicated, may hold values from 0.5 to 2
- gate_weight: bfloat16 [32, 2880, 720], P(('ctx', 'exp')), may hold values from -0.109375 to 0.109375
- up_weight: bfloat16 [32, 2880, 720], P(('ctx', 'exp')), may hold values from -0.109375 to 0.109375
- down_weight: bfloat16 [32, 720, 2880], P(('ctx', 'exp')), may hold values from -0.15625 to 0.15625
- expert_ids: int32 [4096, 4], P(('ctx', 'exp')), may hold values from 0 to 15, all different within a row; in each aligned block of 128 rows (0 to 127, 128 to 255, ...) at most 64 rows name the same one
- gate_values: float32 [4096, 4], P(('ctx', 'exp')), may hold values from 0.05 to 0.6
Outputs:
- layer_out: bfloat16 [4096, 2880], P(('ctx', 'exp'))
Inputs may be any that keep to these rules, and one draw needn't show every extreme that they name: `expert_ids`: each row names 4 different experts; among the 128 rows of one device no expert is named more than 64 times.
All inputs are finite; a program needn't handle non-finite values.
Results may differ from a plain program's by a relative error of at most 0.0062.
Values may be sent and summed in bfloat16 or wider, within the bound.
A program may use at most 128 MiB of HBM per device.

v0:
```python
import jax
import jax.numpy as jnp
from jax import lax
from jax.sharding import PartitionSpec as P

HEAD_DIM = 64
WINDOW = 128


block_order = 64
norm_eps = 1e-05
masked_score = -1e30


def passed_along(value, axis, by):
    length = lax.axis_size(axis)
    pairs = [(i, i + by) for i in range(length) if 0 <= i + by < length]
    return lax.ppermute(value, axis, pairs)


def hadamard_table():
    indices = jnp.arange(block_order, dtype=jnp.int32)
    parity = jnp.zeros((block_order, block_order), jnp.int32)
    for bit_level in range(6):
        stride = 2**bit_level
        parity = parity + indices[:, None] // stride % 2 * (indices[None, :] // stride % 2)
    return (1.0 - 2.0 * (parity % 2)).astype(jnp.float32) / 8.0


def rotate_rows(normed):
    row_count, feature_count = normed.shape
    blocks = normed.reshape(row_count, feature_count // block_order, block_order)
    turned = jnp.einsum("tbi,ij->tbj", blocks, hadamard_table(), precision=lax.Precision.HIGHEST)
    return turned.reshape(row_count, feature_count).astype(jnp.bfloat16)


def expert_half(row_block, gate_part, up_part, down_part):
    gate_val = jnp.dot(row_block, gate_part, preferred_element_type=jnp.float32)
    up_val = jnp.dot(row_block, up_part, preferred_element_type=jnp.float32)
    active = (gate_val * jax.nn.sigmoid(1.702 * gate_val) * (up_val + 1.0)).astype(jnp.bfloat16)
    return jnp.dot(active, down_part, preferred_element_type=jnp.float32).astype(jnp.bfloat16)


def attend(query_block, key_block, value_block, sink_logits, query_pos, key_pos):
    scores = jnp.einsum(
        "tkgd,skd->kgts", query_block, key_block, preferred_element_type=jnp.float32
    )
    scores = scores * HEAD_DIM ** (-0.5)
    allowed = (
        (key_pos[None, :] <= query_pos[:, None])
        & (key_pos[None, :] > query_pos[:, None] - WINDOW)
        & (key_pos[None, :] >= 0)
    )
    scores = jnp.where(allowed[None, None], scores, masked_score)
    sink_col = sink_logits.reshape(scores.shape[0], scores.shape[1])[:, :, None]
    largest = jnp.maximum(jnp.max(scores, axis=-1), sink_col)
    weights = jnp.exp(scores - largest[..., None])
    denom_sum = jnp.sum(weights, axis=-1) + jnp.exp(sink_col - largest)
    prob_bf = (weights / denom_sum[..., None]).astype(jnp.bfloat16)
    mixed_out = jnp.einsum(
        "kgts,skd->tkgd", prob_bf, value_block, preferred_element_type=jnp.float32
    )
    return mixed_out.astype(jnp.bfloat16)


def local(
    hidden_in,
    query_rows,
    key_rows,
    value_rows,
    sink_logits,
    out_weight,
    norm_gain,
    gate_weight,
    up_weight,
    down_weight,
    expert_ids,
    gate_values,
):
    row_count, feature_count = hidden_in.shape
    kv_count = key_rows.shape[1] // HEAD_DIM
    head_count = sink_logits.shape[0]
    group_size = head_count // kv_count
    prior_keys, prior_values = passed_along((key_rows, value_rows), ("ctx", "exp"), 1)
    all_keys = jnp.concatenate([prior_keys, key_rows], axis=0).reshape(
        WINDOW + row_count, kv_count, HEAD_DIM
    )
    all_values = jnp.concatenate([prior_values, value_rows], axis=0).reshape(
        WINDOW + row_count, kv_count, HEAD_DIM
    )
    anchor = lax.axis_index(("ctx", "exp")) * row_count
    query_pos = anchor + jnp.arange(row_count, dtype=jnp.int32)
    key_pos = anchor - WINDOW + jnp.arange(WINDOW + row_count, dtype=jnp.int32)
    attended = attend(
        query_rows.reshape(row_count, kv_count, group_size, HEAD_DIM),
        all_keys,
        all_values,
        sink_logits,
        query_pos,
        key_pos,
    )
    attended = attended.reshape(row_count, head_count * HEAD_DIM)
    mid_stream = hidden_in.astype(jnp.float32) + jnp.dot(
        attended, out_weight, preferred_element_type=jnp.float32
    )
    normed = (
        mid_stream
        * lax.rsqrt(jnp.mean(mid_stream * mid_stream, axis=-1, keepdims=True) + norm_eps)
        * norm_gain
    )
    rotated = rotate_rows(normed)
    top_count = expert_ids.shape[1]
    route_ids = expert_ids.reshape(-1)
    route_total = route_ids.shape[0]
    device_count = lax.axis_size("ctx") * lax.axis_size("exp")
    expert_total = device_count // 2
    capacity = max(2, 2 * route_total // expert_total)
    chosen = (route_ids[:, None] == jnp.arange(expert_total, dtype=jnp.int32)[None, :]).astype(
        jnp.float32
    )
    route_axis = jnp.arange(route_total, dtype=jnp.int32)
    earlier = (route_axis[:, None] > route_axis[None, :]).astype(jnp.float32)
    rank_list = jnp.sum(
        jnp.dot(earlier, chosen, preferred_element_type=jnp.float32) * chosen, axis=1
    ).astype(jnp.int32)
    slot_index = route_ids * capacity + rank_list
    source_rows = jnp.repeat(rotated, top_count, axis=0)
    packed = (
        jnp.zeros((expert_total * capacity, feature_count), jnp.bfloat16)
        .at[slot_index]
        .set(source_rows)
    )
    outgoing = jnp.repeat(packed.reshape(expert_total, 1, capacity, feature_count), 2, axis=1)
    outgoing = outgoing.reshape(device_count, capacity, feature_count)
    arrived = lax.all_to_all(outgoing, ("ctx", "exp"), split_axis=0, concat_axis=0, tiled=True)
    flat_rows = arrived.reshape(-1, feature_count)
    produced = expert_half(flat_rows, gate_weight[0], up_weight[0], down_weight[0])
    returned = lax.all_to_all(
        produced.reshape(arrived.shape), ("ctx", "exp"), split_axis=0, concat_axis=0, tiled=True
    )
    both_halves = returned.reshape(expert_total, 2, capacity, feature_count)
    summed = (
        both_halves[:, 0].astype(jnp.float32) + both_halves[:, 1].astype(jnp.float32)
    ).reshape(expert_total * capacity, feature_count)
    picked = summed[slot_index] * gate_values.reshape(-1)[:, None]
    expert_sum = jnp.sum(picked.reshape(row_count, top_count, feature_count), axis=1)
    return (mid_stream + expert_sum).astype(jnp.bfloat16)


def solution(mesh):
    in_specs = (
        P(("ctx", "exp"), None),
        P(("ctx", "exp"), None),
        P(("ctx", "exp"), None),
        P(("ctx", "exp"), None),
        P(),
        P(),
        P(),
        P(("ctx", "exp"), None, None),
        P(("ctx", "exp"), None, None),
        P(("ctx", "exp"), None, None),
        P(("ctx", "exp"), None),
        P(("ctx", "exp"), None),
    )
    out_specs = P(("ctx", "exp"), None)
    return jax.shard_map(local, mesh=mesh, in_specs=in_specs, out_specs=out_specs, check_vma=False)
```

profile of v0, /device:TPU:14, one launch (start us, length us, event | category | flops | bytes accessed | tf_op | source)
XLA Modules:
  0.0 677.9 jit_solution(4373105037749378509)
XLA Ops:
  0.0 1.9 collective-permute-start.1
  1.9 3.5 collective-permute-start
  5.5 0.8 copy.37
  6.3 0.7 broadcast_multiply_fusion
  7.0 1.3 copy.34
  8.3 0.7 max.17
  9.8 0.9 pad_maximum_fusion.1
  10.8 0.8 fusion.8
  11.6 1.8 copy-done
  13.5 0.9 fusion.7
  14.7 3.4 fusion.14
  18.1 6.3 multiply_reduce_fusion.1
  24.5 1.1 copy-done.2
  26.0 1.4 convolution_convert_fusion.1
  27.5 1.2 copy.38
  28.6 1.9 broadcast_in_dim.21
  30.5 2.9 reshape.770
  33.4 9.5 %scatter_custom_fusion = bf16[1024,2880]{1,0:T(8,128)(2,1)} fusion(s32[512]{0:T(512)S(1)} %bitcast.78, bf16[512,2880]{1,0:T(8,128)(2,1)} %reshape.770, bf16[]{:T(256)} %constant.238.clone.1), kind=kCustom, calls=%fused_computation.19 | custom fusion | bytes 5898752 | tf_op jit(solution)/shard_map/scatter | solution.py:131
  43.0 5.3 broadcast_in_dim.22
  48.3 265.5 %all_to_all.10 = bf16[32,64,2880]{2,1,0:T(8,128)(2,1)S(1)} all-to-all(bf16[32,64,2880]{2,1,0:T(8,128)(2,1)S(1)} %bitcast.69), channel_id=1, replica_groups=mesh['ctx'=4,'exp'=8] {'ctx','exp'}, dimensions={0} | all-to-all | bytes 23592960 | tf_op jit(solution)/shard_map/all_to_all | solution.py:135
  313.7 4.3 copy-done.1
  318.0 11.1 %fusion.1 = f32[2048,720]{0,1:T(8,128)} fusion(bf16[2048,2880]{1,0:T(8,128)(2,1)S(1)} %bitcast.71, bf16[1,2880,720]{1,2,0:T(8,128)(2,1)S(1)} %bitcast.82), kind=kOutput, calls=%fused_computation.9 | convolution fusion | flops 8493465600 | bytes 21841920 | tf_op jit(solution)/shard_map/dot_general | solution.py:39
  329.1 26.6 %convolution_convert_fusion = bf16[2048,2880]{0,1:T(8,128)(2,1)} fusion(bf16[1,720,2880]{2,1,0:T(8,128)(2,1)} %param.21, f32[2048,720]{0,1:T(8,128)} %fusion.1, bf16[2048,2880]{1,0:T(8,128)(2,1)} %bitcast.72, bf16[1,2880,720]{1,2,0:T(8,128)(2,1)} %param.19), kind=kOutput, calls=%fused_computation.3 | convolution fusion | flops 17004625920 | bytes 37785600 | tf_op jit(solution)/shard_map/dot_general | solution.py:41
  355.7 16.4 %copy.39 = bf16[2048,2880]{1,0:T(8,128)(2,1)} copy(bf16[2048,2880]{0,1:T(8,128)(2,1)} %convolution_convert_fusion) | data formatting | bytes 23592960 | tf_op jit(solution)/shard_map/convert_element_type | solution.py:41
  372.1 5.9 all-to-all-start.1
  378.1 259.4 %all-to-all-done.1 = bf16[32,64,2880]{2,1,0:T(8,128)(2,1)} async-done(((bf16[32,64,2880]{2,1,0:T(8,128)(2,1)}), bf16[32,64,2880]{2,1,0:T(8,128)(2,1)}, u32[]{:S(2)}, u32[]{:S(2)}) %all-to-all-start.1) | async-done | bytes 11796512 | tf_op jit(solution)/shard_map/all_to_all | solution.py:138
  637.5 10.2 %convert_add_fusion = f32[16,1,64,2880]{3,2,0,1:T(8,128)} fusion(bf16[16,2,64,2880]{3,2,1,0:T(8,128)(2,1)} %bitcast.22), kind=kLoop, calls=%fused_computation.2 | loop fusion | flops 8847360 | bytes 23592960 | tf_op jit(solution)/shard_map/add | solution.py:143
  647.7 11.4 %gather_fusion = f32[512,2880]{1,0:T(8,128)} fusion(f32[1024,2880]{1,0:T(8,128)} %bitcast.67, s32[1024]{0:T(1024)S(1)} %pad_clamp_fusion), kind=kCustom, calls=%fused_computation | custom fusion | bytes 11798528 | tf_op jit(solution)/shard_map/gather | solution.py:145
  659.1 7.7 %gather.6 = f32[128,4,2880]{2,1,0:T(4,128)} reshape(f32[512,2880]{1,0:T(8,128)} %gather_fusion) | data formatting | bytes 11796480 | tf_op jit(solution)/shard_map/gather | solution.py:145
  666.8 7.1 %multiply_reduce_fusion = f32[128,2880]{1,0:T(8,128)S(1)} fusion(f32[128,4,2880]{2,1,0:T(4,128)} %gather.6, f32[128,4]{1,0:T(8,128)S(1)} %copy.42), kind=kLoop, calls=%fused_computation.6 | loop fusion | flops 2580480 | bytes 7374848 | tf_op jit(solution)/shard_map/reduce_sum | solution.py:146
  673.9 1.6 copy.43
  675.5 2.4 add_convert_fusion
  (42 shorter events, 1.8 us)
Async XLA Ops:
  0.0 9.8 %collective-permute-start.1 = (bf16[128,256]{1,0:T(8,128)(2,1)}, bf16[128,256]{1,0:T(8,128)(2,1)S(1)}, u32[]{:S(2)}, u32[]{:S(2)}) collective-permute-start(bf16[128,256]{1,0:T(8,128)(2,1)} %param.14), channel_id=1, source_target_pairs={{0,1},{1,2},{2,3},{3,4},{4,5},{5,6},{6,7},{7,8},{8,9},{9,10},{10,1... | collective-permute-start | bytes 196616 | tf_op jit(solution)/shard_map/ppermute | solution.py:18
  1.9 12.6 %collective-permute-start = (bf16[128,256]{1,0:T(8,128)(2,1)}, bf16[128,256]{1,0:T(8,128)(2,1)S(1)}, u32[]{:S(2)}, u32[]{:S(2)}) collective-permute-start(bf16[128,256]{1,0:T(8,128)(2,1)} %param.15), channel_id=1, source_target_pairs={{0,1},{1,2},{2,3},{3,4},{4,5},{5,6},{6,7},{7,8},{8,9},{9,10},{10,1... | collective-permute-start | bytes 196616 | tf_op jit(solution)/shard_map/ppermute | solution.py:18
  10.8 3.7 copy-start.4
  11.6 1.9 copy-start
  14.6 3.4 copy-start.7
  18.1 7.5 %copy-start.5 = (f32[2880]{0:T(1024)S(1)}, f32[2880]{0:T(1024)}, u32[]{:S(2)}) copy-start(f32[2880]{0:T(1024)} %param.18) | copy-start | bytes 34564
  24.4 1.1 copy-start.2
  43.0 275.1 %slice-start = ((s8[4239360]{0:T(1024)(128)(4,1)}), s8[4194304]{0:T(1024)(128)(4,1)S(1)}, s32[]{:S(2)}) async-start(s8[4239360]{0:T(1024)(128)(4,1)} %bitcast.81), calls=%async_computation.2 | async-start | bytes 8388608
  48.2 269.8 %slice-start.1 = ((s8[4239360]{0:T(1024)(128)(4,1)}), s8[45056]{0:T(1024)(128)(4,1)S(1)}, s32[]{:S(2)}) async-start(s8[4239360]{0:T(1024)(128)(4,1)} %bitcast.81), calls=%async_computation.3 | async-start | bytes 90112
  313.7 4.3 copy-start.1
  372.1 5.9 copy-start.6
  372.1 265.4 %all-to-all-start.1 = ((bf16[32,64,2880]{2,1,0:T(8,128)(2,1)}), bf16[32,64,2880]{2,1,0:T(8,128)(2,1)}, u32[]{:S(2)}, u32[]{:S(2)}) async-start(bf16[32,64,2880]{2,1,0:T(8,128)(2,1)} %bitcast.68), calls=%async_computation.1 | async-start | bytes 24117248 | tf_op jit(solution)/shard_map/all_to_all | solution.py:138
  666.8 8.7 %copy-start.3 = (f32[128,2880]{0,1:T(8,128)S(1)}, f32[128,2880]{0,1:T(8,128)}, u32[]{:S(2)}) copy-start(f32[128,2880]{0,1:T(8,128)} %copy-done.2) | copy-start | bytes 4423684
where the time goes:
time: 688 us; the launch traced here: 678 us
  blocking collectives  265 us (39%)
  waiting for transfers between devices  259 us (38%)
  local copies, waits for them, and re-layouts  68.6 us (10%)
  matrix products  49.9 us (7%)
  other arithmetic  23 us (3%)
  starting transfers between devices  11.3 us (2%)
    all_to_all x1, blocking collectives, local(): lax.all_to_all(outgoing, ('ctx', 'exp'), split_axis=0, concat_axis=0, til...  265 us
    all_to_all x1, waiting for transfers between devices, local(): lax.all_to_all(produced.reshape(arrived.shape), ('ctx', 'exp'), split_axi...  259 us
    dot_general x1, matrix products, expert_half(): jnp.dot(active, down_part, preferred_element_type=jnp.float32)  26.6 us
    gather x2, local copies, waits for them, and re-layouts, local(): picked = summed[slot_index] * gate_values.reshape(-1)[:, None]  19.1 us
    convert_element_type x1, local copies, waits for them, and re-layouts, expert_half(): jnp.dot(active, down_part, preferred_element_type=jnp.float32)  16.4 us
  transfers between devices with their start and end apart: 3, of which 1 were waited for; matrix products, arithmetic and copies ran while one was open for 1% of the time, Pallas kernels for 0%

commit v1 on v0

v1 whole, which is shorter than its diff:
```python
import jax
import jax.numpy as jnp
from jax import lax
from jax.experimental import pallas as pl
from jax.experimental.pallas import tpu as pltpu
from jax.sharding import Mesh, PartitionSpec as P

HEAD_DIM = 64
WINDOW = 128


AXES = ("ctx", "chip", "core")
CHIPS = ("ctx", "chip")

block_order = 64
norm_eps = 1e-05
masked_score = -1e30


def passed_along(value, axis, by):
    length = lax.axis_size(axis)
    pairs = [(i, i + by) for i in range(length) if 0 <= i + by < length]
    return lax.ppermute(value, axis, pairs)


def hadamard_table():
    indices = jnp.arange(block_order, dtype=jnp.int32)
    parity = jnp.zeros((block_order, block_order), jnp.int32)
    for bit_level in range(6):
        stride = 2**bit_level
        parity = parity + indices[:, None] // stride % 2 * (indices[None, :] // stride % 2)
    return (1.0 - 2.0 * (parity % 2)).astype(jnp.float32) / 8.0


def rotate_rows(normed):
    row_count, feature_count = normed.shape
    blocks = normed.reshape(row_count, feature_count // block_order, block_order)
    turned = jnp.einsum("tbi,ij->tbj", blocks, hadamard_table(), precision=lax.Precision.HIGHEST)
    return turned.reshape(row_count, feature_count).astype(jnp.bfloat16)


def ffn_body(row_ref, gate_ref, up_ref, down_ref, out_ref):
    rows = row_ref[...]
    gate_val = jnp.dot(rows, gate_ref[0], preferred_element_type=jnp.float32)
    up_val = jnp.dot(rows, up_ref[0], preferred_element_type=jnp.float32)
    active = (gate_val * jax.nn.sigmoid(1.702 * gate_val) * (up_val + 1.0)).astype(jnp.bfloat16)
    out_ref[...] = jnp.dot(active, down_ref[0], preferred_element_type=jnp.float32).astype(
        out_ref.dtype
    )


def expert_half(row_block, gate_part, up_part, down_part):
    row_total, feature_count = row_block.shape
    tile = 256

    def whole(part):
        return pl.BlockSpec(part.shape, lambda i: (0, 0, 0), pipeline_mode=pl.Buffered(1))

    def rows():
        return pl.BlockSpec((tile, feature_count), lambda i: (i, 0))

    weight_count = gate_part.size + up_part.size + down_part.size
    return pl.pallas_call(
        ffn_body,
        out_shape=jax.ShapeDtypeStruct(row_block.shape, jnp.bfloat16),
        grid=(row_total // tile,),
        in_specs=[rows(), whole(gate_part), whole(up_part), whole(down_part)],
        out_specs=rows(),
        compiler_params=pltpu.CompilerParams(vmem_limit_bytes=40 << 20),
        cost_estimate=pl.CostEstimate(
            flops=2 * row_total * weight_count,
            bytes_accessed=2 * weight_count + 4 * row_total * feature_count,
            transcendentals=row_total * gate_part.shape[2],
        ),
    )(row_block, gate_part, up_part, down_part)


def attend(query_block, key_block, value_block, sink_logits, query_pos, key_pos):
    scores = jnp.einsum(
        "tkgd,skd->kgts", query_block, key_block, preferred_element_type=jnp.float32
    )
    scores = scores * HEAD_DIM ** (-0.5)
    allowed = (
        (key_pos[None, :] <= query_pos[:, None])
        & (key_pos[None, :] > query_pos[:, None] - WINDOW)
        & (key_pos[None, :] >= 0)
    )
    scores = jnp.where(allowed[None, None], scores, masked_score)
    sink_col = sink_logits.reshape(scores.shape[0], scores.shape[1])[:, :, None]
    largest = jnp.maximum(jnp.max(scores, axis=-1), sink_col)
    weights = jnp.exp(scores - largest[..., None])
    denom_sum = jnp.sum(weights, axis=-1) + jnp.exp(sink_col - largest)
    prob_bf = (weights / denom_sum[..., None]).astype(jnp.bfloat16)
    mixed_out = jnp.einsum(
        "kgts,skd->tkgd", prob_bf, value_block, preferred_element_type=jnp.float32
    )
    return mixed_out.astype(jnp.bfloat16)


def local(
    hidden_in,
    query_rows,
    key_rows,
    value_rows,
    sink_logits,
    out_weight,
    norm_gain,
    gate_weight,
    up_weight,
    down_weight,
    expert_ids,
    gate_values,
):
    row_count, feature_count = hidden_in.shape
    slot_hot, slot_gate = route_tables(expert_ids, gate_values, lax.axis_size(CHIPS))
    kv_count = key_rows.shape[1] // HEAD_DIM
    head_count = sink_logits.shape[0]
    group_size = head_count // kv_count
    prior_keys, prior_values = passed_along((key_rows, value_rows), AXES, 1)
    all_keys = jnp.concatenate([prior_keys, key_rows], axis=0).reshape(
        WINDOW + row_count, kv_count, HEAD_DIM
    )
    all_values = jnp.concatenate([prior_values, value_rows], axis=0).reshape(
        WINDOW + row_count, kv_count, HEAD_DIM
    )
    anchor = lax.axis_index(AXES) * row_count
    query_pos = anchor + jnp.arange(row_count, dtype=jnp.int32)
    key_pos = anchor - WINDOW + jnp.arange(WINDOW + row_count, dtype=jnp.int32)
    attended = attend(
        query_rows.reshape(row_count, kv_count, group_size, HEAD_DIM),
        all_keys,
        all_values,
        sink_logits,
        query_pos,
        key_pos,
    )
    attended = attended.reshape(row_count, head_count * HEAD_DIM)
    mid_stream = hidden_in.astype(jnp.float32) + jnp.dot(
        attended, out_weight, preferred_element_type=jnp.float32
    )
    normed = (
        mid_stream
        * lax.rsqrt(jnp.mean(mid_stream * mid_stream, axis=-1, keepdims=True) + norm_eps)
        * norm_gain
    )
    rotated = rotate_rows(normed)
    packed = jnp.dot(
        slot_hot.astype(jnp.bfloat16).T, rotated, preferred_element_type=jnp.float32
    ).astype(jnp.bfloat16)
    expert_total = lax.axis_size(CHIPS)
    outgoing = packed.reshape(expert_total, -1, feature_count)
    arrived = lax.all_to_all(outgoing, CHIPS, split_axis=0, concat_axis=0, tiled=True)
    mine = arrived.reshape(-1, feature_count)
    swap = [(0, 1), (1, 0)]
    theirs = lax.ppermute(mine, "core", swap)
    made_mine = expert_half(mine, gate_weight, up_weight, down_weight)
    made_theirs = expert_half(theirs, gate_weight, up_weight, down_weight)
    other_half = lax.ppermute(made_theirs, "core", swap)
    summed = (made_mine.astype(jnp.float32) + other_half.astype(jnp.float32)).astype(jnp.bfloat16)
    returned = lax.all_to_all(
        summed.reshape(arrived.shape), CHIPS, split_axis=0, concat_axis=0, tiled=True
    ).reshape(-1, feature_count)
    gate_high = lax.reduce_precision(slot_gate, 8, 7)
    gate_parts = jnp.concatenate([gate_high, slot_gate - gate_high], axis=0).astype(jnp.bfloat16)
    weighted = jnp.dot(gate_parts, returned, preferred_element_type=jnp.float32)
    expert_sum = weighted[:row_count] + weighted[row_count:]
    return (mid_stream + expert_sum).astype(jnp.bfloat16)


def route_tables(expert_ids, gate_values, expert_total):
    row_count, top_count = expert_ids.shape
    capacity = max(2, 2 * row_count * top_count // expert_total)
    experts = jnp.arange(expert_total, dtype=jnp.int32)
    named = expert_ids[:, :, None] == experts[None, None, :]
    chosen = jnp.any(named, axis=1).astype(jnp.float32)
    row_axis = jnp.arange(row_count, dtype=jnp.int32)
    earlier = (row_axis[:, None] > row_axis[None, :]).astype(jnp.float32)
    rank = jnp.dot(earlier, chosen, preferred_element_type=jnp.float32)
    route_rank = jnp.sum(jnp.where(named, rank[:, None, :], 0.0), axis=2).astype(jnp.int32)
    slot = expert_ids * capacity + route_rank
    slots = jnp.arange(expert_total * capacity, dtype=jnp.int32)
    slot_hot = jnp.zeros((row_count, slots.shape[0]), jnp.float32)
    slot_gate = slot_hot
    for k in range(top_count):
        here = slot[:, k : k + 1] == slots[None, :]
        slot_hot = jnp.where(here, 1.0, slot_hot)
        slot_gate = jnp.where(here, gate_values[:, k : k + 1], slot_gate)
    return slot_hot, slot_gate


def solution(mesh):
    ctx_size, exp_size = mesh.devices.shape
    mesh = Mesh(mesh.devices.reshape(ctx_size, exp_size // 2, 2), AXES)
    in_specs = (
        P(AXES, None),
        P(AXES, None),
        P(AXES, None),
        P(AXES, None),
        P(),
        P(),
        P(),
        P(AXES, None, None),
        P(AXES, None, None),
        P(AXES, None, None),
        P(AXES, None),
        P(AXES, None),
    )
    out_specs = P(AXES, None)
    return jax.shard_map(local, mesh=mesh, in_specs=in_specs, out_specs=out_specs, check_vma=False)
```

time: 688 us -> 435 us (0.63); the launches traced: 678 us -> 433 us
  blocking collectives: 265 us -> 137 us
  waiting for transfers between devices: 259 us -> 137 us
  Pallas kernels: 0 us -> 35.8 us
  matrix products: 49.9 us -> 21.5 us
  other arithmetic: 23 us -> 14.8 us
    all_to_all x1, blocking collectives: 265 us -> 137 us  [local(): lax.all_to_all(outgoing, CHIPS, split_axis=0, concat_axis=0, tiled=True)]
    all_to_all x1, waiting for transfers between devices: 259 us -> 137 us  [local(): lax.all_to_all(summed.reshape(arrived.shape), CHIPS, split_axis=0, concat...]
    pallas_call x0 -> x2, Pallas kernels: none -> 35.8 us  [expert_half(): pl.pallas_call(ffn_body, out_shape=jax.ShapeDtypeStruct(row_block.shape,...]
    dot_general x3, matrix products: 37.9 us -> 9.77 us  [the longest x1 5.25 us: local(): weighted = jnp.dot(gate_parts, returned, preferred_element_type=jnp.float32)]
    unnamed x23 -> x25, local copies, waits for them, and re-layouts: 9.51 us -> 30 us
    gather x2 -> x0, local copies, waits for them, and re-layouts: 19.1 us -> none  [local(): picked = summed[slot_index] * gate_values.reshape(-1)[:, None]]
    ppermute x0 -> x2, local copies, waits for them, and re-layouts: none -> 17 us  [the longest x1 8.5 us: local(): other_half = lax.ppermute(made_theirs, 'core', swap)]
    scatter x1 -> x0, local copies, waits for them, and re-layouts: 9.55 us -> none  [local(): packed = jnp.zeros((expert_total * capacity, feature_count), jnp.bfloat16...]
  transfers between devices with their start and end apart: 3 -> 5, of which waited for: 1 -> 1; matrix products, arithmetic and copies ran while one was open for 1% -> 5% of each run, Pallas kernels for 0% -> 4%
where the time goes in v1:
time: 435 us; the launch traced here: 433 us
  waiting for transfers between devices  137 us (31%)
  blocking collectives  137 us (31%)
  local copies, waits for them, and re-layouts  73.3 us (17%)
  Pallas kernels  35.8 us (8%)
  matrix products  21.5 us (5%)
  other arithmetic  14.8 us (3%)
  starting transfers between devices  13.2 us (3%)
    all_to_all x1, blocking collectives, local(): lax.all_to_all(outgoing, CHIPS, split_axis=0, concat_axis=0, tiled=True)  137 us
    all_to_all x1, waiting for transfers between devices, local(): lax.all_to_all(summed.reshape(arrived.shape), CHIPS, split_axis=0, concat...  137 us
    pallas_call x2, Pallas kernels, expert_half(): pl.pallas_call(ffn_body, out_shape=jax.ShapeDtypeStruct(row_block.shape,...  35.8 us
    unnamed x25, local copies, waits for them, and re-layouts  30 us
  transfers between devices with their start and end apart: 5, of which 1 were waited for; matrix products, arithmetic and copies ran while one was open for 5% of the time, Pallas kernels for 4%

profile of v1, /device:TPU:14, one launch (start us, length us, event | category | flops | bytes accessed | tf_op | source)
XLA Modules:
  0.0 433.4 jit_solution(222246464070729738)
XLA Ops:
  0.0 1.9 collective-permute-start.1
  1.9 3.5 collective-permute-start
  5.5 1.3 copy.52
  10.0 0.9 pad_maximum_fusion.1
  10.9 0.8 fusion.1
  11.8 1.9 copy-done.6
  13.7 0.9 fusion
  14.8 3.4 fusion.5
  18.3 6.1 %multiply_reduce_fusion = (f32[128]{0:T(128)S(1)}, f32[128,2880]{0,1:T(8,128)S(1)}) fusion(bf16[2048,2880]{0,1:T(8,128)(2,1)} %param.17, bf16[128,2048]{0,1:T(8,128)(2,1)S(1)} %bitcast.68, bf16[128,2880]{0,1:T(8,128)(2,1)S(1)} %copy-done.10), kind=kOutput, calls=%fused_computation.13 | convolution fusion | flops 1511423872 | bytes 14533120 | tf_op jit(solution)/shard_map/dot_general | solution.py:138
  24.9 1.4 convolution_convert_fusion.1
  26.3 4.4 %convolution_convert_fusion = bf16[1024,2880]{0,1:T(8,128)(2,1)} fusion(bf16[128,2880]{0,1:T(8,128)(2,1)S(1)} %bitcast.64, s32[128]{0:T(128)S(1)} %get-tuple-element.12, s32[128]{0:T(128)S(1)} %get-tuple-element.13, s32[128]{0:T(128)S(1)} %get-tuple-element.14, s32[128]{0:T(128)S(1)} %get-tuple-element.11), kind=kOutput, calls=%fused_computation.1 | convolution fusion | flops 759103488 | bytes 6637568 | tf_op jit(solution)/shard_map/dot_general | solution.py:147
  30.7 8.5 %copy.54 = bf16[1024,2880]{1,0:T(8,128)(2,1)} copy(bf16[1024,2880]{0,1:T(8,128)(2,1)} %convolution_convert_fusion) | data formatting | bytes 11796480 | tf_op jit(solution)/shard_map/convert_element_type | solution.py:149
  39.2 137.5 %all_to_all.10 = bf16[16,64,2880]{2,1,0:T(8,128)(2,1)} all-to-all(bf16[16,64,2880]{2,1,0:T(8,128)(2,1)} %bitcast.62), channel_id=1, replica_groups=mesh['ctx'=4,'chip'=4,'core'=2] {'ctx','chip'}, dimensions={0} | all-to-all | bytes 11796480 | tf_op jit(solution)/shard_map/all_to_all | solution.py:152
  176.7 8.4 %copy.57 = bf16[1024,2880]{0,1:T(8,128)(2,1)} copy(bf16[1024,2880]{1,0:T(8,128)(2,1)} %bitcast.60) | data formatting | bytes 11796480 | tf_op jit(solution)/shard_map/reshape | solution.py:153
  185.2 6.7 %copy.55.gate_ref = bf16[1,2880,720]{2,1,0:T(8,128)(2,1)} copy(bf16[1,2880,720]{1,2,0:T(8,128)(2,1)} %param.19) | data formatting | bytes 8294400 | tf_op args[7]
  191.9 6.7 %copy.56.up_ref = bf16[1,2880,720]{2,1,0:T(8,128)(2,1)} copy(bf16[1,2880,720]{1,2,0:T(8,128)(2,1)} %param.20) | data formatting | bytes 8294400 | tf_op args[8]
  198.5 8.5 %copy.58.row_ref = bf16[1024,2880]{1,0:T(8,128)(2,1)} copy(bf16[1024,2880]{0,1:T(8,128)(2,1)} %collective-permute-done.2) | data formatting | bytes 11796480 | tf_op jit(solution)/shard_map/ppermute | solution.py:155
  207.0 2.3 copy-done
  209.2 2.3 copy-done.2
  211.5 2.2 copy-done.4
  213.7 17.9 %shard_map.119 = bf16[1024,2880]{1,0:T(8,128)(2,1)} custom-call(bf16[1024,2880]{1,0:T(8,128)(2,1)} %copy.58.row_ref, bf16[1,2880,720]{2,1,0:T(8,128)(2,1)S(1)} %copy-done, bf16[1,2880,720]{2,1,0:T(8,128)(2,1)S(1)} %copy-done.2, bf16[1,720,2880]{2,1,0:T(8,128)(2,1)S(1)} %copy-done.4), custom_call_target="tpu_custom_call" | custom-call | flops 12740198400 | bytes 24238080 | tf_op jit(solution)/shard_map/pallas_call | solution.py:63
  231.6 8.4 %copy.61 = bf16[1024,2880]{0,1:T(8,128)(2,1)} copy(bf16[1024,2880]{1,0:T(8,128)(2,1)} %shard_map.119) | data formatting | bytes 11796480 | tf_op jit(solution)/shard_map/pallas_call | solution.py:63
  240.5 2.3 copy-done.1
  242.8 2.3 copy-done.3
  245.1 2.2 copy-done.5
  247.3 17.9 %shard_map.118 = bf16[1024,2880]{1,0:T(8,128)(2,1)} custom-call(bf16[1024,2880]{1,0:T(8,128)(2,1)} %bitcast.61, bf16[1,2880,720]{2,1,0:T(8,128)(2,1)S(1)} %copy-done.1, bf16[1,2880,720]{2,1,0:T(8,128)(2,1)S(1)} %copy-done.3, bf16[1,720,2880]{2,1,0:T(8,128)(2,1)S(1)} %copy-done.5), custom_call_target="tpu_custom_call" | custom-call | flops 12740198400 | bytes 24238080 | tf_op jit(solution)/shard_map/pallas_call | solution.py:63
  265.1 8.5 %copy.62 = bf16[1024,2880]{1,0:T(8,128)(2,1)} copy(bf16[1024,2880]{0,1:T(8,128)(2,1)} %collective-permute-done.3) | data formatting | bytes 11796480 | tf_op jit(solution)/shard_map/ppermute | solution.py:158
  273.6 8.5 %add_convert_fusion = bf16[1024,2880]{1,0:T(8,128)(2,1)} fusion(bf16[1024,2880]{1,0:T(8,128)(2,1)} %copy.62, bf16[1024,2880]{1,0:T(8,128)(2,1)} %shard_map.118), kind=kLoop, calls=%fused_computation | loop fusion | flops 11796480 | bytes 17694720 | tf_op jit(solution)/shard_map/convert_element_type | solution.py:159
  282.1 7.3 %all-to-all-start.1 = ((bf16[16,64,2880]{2,1,0:T(8,128)(2,1)}), bf16[16,64,2880]{2,1,0:T(8,128)(2,1)}, u32[]{:S(2)}, u32[]{:S(2)}) async-start(bf16[16,64,2880]{2,1,0:T(8,128)(2,1)} %bitcast.59), calls=%async_computation.1 | async-start | bytes 12058624 | tf_op jit(solution)/shard_map/all_to_all | solution.py:160
  289.9 137.0 %all-to-all-done.1 = bf16[16,64,2880]{2,1,0:T(8,128)(2,1)} async-done(((bf16[16,64,2880]{2,1,0:T(8,128)(2,1)}), bf16[16,64,2880]{2,1,0:T(8,128)(2,1)}, u32[]{:S(2)}, u32[]{:S(2)}) %all-to-all-start.1) | async-done | bytes 5898272 | tf_op jit(solution)/shard_map/all_to_all | solution.py:160
  426.9 5.3 %fusion.7 = f32[256,2880]{0,1:T(8,128)S(1)} fusion(bf16[1024,2880]{1,0:T(8,128)(2,1)} %bitcast.24, bf16[128,1024]{1,0:T(8,128)(2,1)S(1)} %get-tuple-element.6, bf16[128,1024]{1,0:T(8,128)(2,1)S(1)} %get-tuple-element.5), kind=kOutput, calls=%fused_computation.19 | convolution fusion | flops 1510998016 | bytes 9371648 | tf_op jit(solution)/shard_map/dot_general | solution.py:165
  432.2 1.2 fusion.4
  (43 shorter events, 4.9 us)
Async XLA Ops:
  0.0 10.0 %collective-permute-start.1 = (bf16[128,256]{1,0:T(8,128)(2,1)}, bf16[128,256]{1,0:T(8,128)(2,1)S(1)}, u32[]{:S(2)}, u32[]{:S(2)}) collective-permute-start(bf16[128,256]{1,0:T(8,128)(2,1)} %param.14), channel_id=1, source_target_pairs={{0,1},{1,2},{2,3},{3,4},{4,5},{5,6},{6,7},{7,8},{8,9},{9,10},{10,1... | collective-permute-start | bytes 196616 | tf_op jit(solution)/shard_map/ppermute | solution.py:23
  1.9 12.8 %collective-permute-start = (bf16[128,256]{1,0:T(8,128)(2,1)}, bf16[128,256]{1,0:T(8,128)(2,1)S(1)}, u32[]{:S(2)}, u32[]{:S(2)}) collective-permute-start(bf16[128,256]{1,0:T(8,128)(2,1)} %param.15), channel_id=1, source_target_pairs={{0,1},{1,2},{2,3},{3,4},{4,5},{5,6},{6,7},{7,8},{8,9},{9,10},{10,1... | collective-permute-start | bytes 196616 | tf_op jit(solution)/shard_map/ppermute | solution.py:23
  10.9 3.7 copy-start.7
  11.7 2.0 copy-start.6
  14.8 3.4 copy-start.10
  18.3 6.2 %copy-start.8 = (f32[2880]{0:T(1024)S(1)}, f32[2880]{0:T(1024)}, u32[]{:S(2)}) copy-start(f32[2880]{0:T(1024)} %param.18) | copy-start | bytes 34564
  185.1 13.4 %collective-permute-start.2 = (bf16[1024,2880]{0,1:T(8,128)(2,1)}, bf16[1024,2880]{0,1:T(8,128)(2,1)}, u32[]{:S(2)}, u32[]{:S(2)}) collective-permute-start(bf16[1024,2880]{0,1:T(8,128)(2,1)} %copy.57), channel_id=1, source_target_pairs={{0,1},{1,0},{2,3},{3,2},{4,5},{5,4},{6,7},{7,6},{8,9},{9,8},{10,11... | collective-permute-start | bytes 17694728 | tf_op jit(solution)/shard_map/ppermute | solution.py:155
  207.0 2.3 copy-start
  209.2 2.3 copy-start.2
  211.5 2.2 copy-start.4
  240.0 25.1 %collective-permute-start.3 = (bf16[1024,2880]{0,1:T(8,128)(2,1)}, bf16[1024,2880]{0,1:T(8,128)(2,1)}, u32[]{:S(2)}, u32[]{:S(2)}) collective-permute-start(bf16[1024,2880]{0,1:T(8,128)(2,1)} %copy.61), channel_id=1, source_target_pairs={{0,1},{1,0},{2,3},{3,2},{4,5},{5,4},{6,7},{7,6},{8,9},{9,8},{10,11... | collective-permute-start | bytes 17694728 | tf_op jit(solution)/shard_map/ppermute | solution.py:158
  240.5 2.3 copy-start.1
  242.8 2.3 copy-start.3
  245.1 2.2 copy-start.5
  282.1 7.3 %copy-start.9 = (f32[128,4]{0,1:T(4,128)S(1)}, f32[128,4]{0,1:T(4,128)}, u32[]{:S(2)}) copy-start(f32[128,4]{0,1:T(4,128)} %param.23) | copy-start | bytes 6148
  282.1 144.8 %all-to-all-start.1 = ((bf16[16,64,2880]{2,1,0:T(8,128)(2,1)}), bf16[16,64,2880]{2,1,0:T(8,128)(2,1)}, u32[]{:S(2)}, u32[]{:S(2)}) async-start(bf16[16,64,2880]{2,1,0:T(8,128)(2,1)} %bitcast.59), calls=%async_computation.1 | async-start | bytes 12058624 | tf_op jit(solution)/shard_map/all_to_all | solution.py:160

commit v2 on v1

--- a/solution.py
+++ b/solution.py
@@ -11,6 +11,7 @@
 
 AXES = ("ctx", "chip", "core")
 CHIPS = ("ctx", "chip")
+CHUNKS = 2
 
 block_order = 64
 norm_eps = 1e-05
@@ -39,18 +40,25 @@
     return turned.reshape(row_count, feature_count).astype(jnp.bfloat16)
 
 
-def ffn_body(row_ref, gate_ref, up_ref, down_ref, out_ref):
-    rows = row_ref[...]
-    gate_val = jnp.dot(rows, gate_ref[0], preferred_element_type=jnp.float32)
-    up_val = jnp.dot(rows, up_ref[0], preferred_element_type=jnp.float32)
-    active = (gate_val * jax.nn.sigmoid(1.702 * gate_val) * (up_val + 1.0)).astype(jnp.bfloat16)
-    out_ref[...] = jnp.dot(active, down_ref[0], preferred_element_type=jnp.float32).astype(
-        out_ref.dtype
-    )
-
-
-def expert_half(row_block, gate_part, up_part, down_part):
-    row_total, feature_count = row_block.shape
+def contract_last(rows, part):
+    return lax.dot_general(
+        rows, part, (((1,), (1,)), ((), ())), preferred_element_type=jnp.float32
+    )
+
+
+def ffn_body(mine_ref, theirs_ref, gate_ref, up_ref, down_ref, mine_out, theirs_out):
+    for row_ref, out_ref in ((mine_ref, mine_out), (theirs_ref, theirs_out)):
+        rows = row_ref[...]
+        gate_val = contract_last(rows, gate_ref[0])
+        up_val = contract_last(rows, up_ref[0])
+        active = gate_val * jax.nn.sigmoid(1.702 * gate_val) * (up_val + 1.0)
+        out_ref[...] = jnp.dot(
+            active.astype(jnp.bfloat16), down_ref[0], preferred_element_type=jnp.float32
+        ).astype(out_ref.dtype)
+
+
+def expert_half(mine, theirs, gate_part, up_part, down_part):
+    row_total, feature_count = mine.shape
     tile = 256
 
     def whole(part):
@@ -62,17 +70,44 @@
     weight_count = gate_part.size + up_part.size + down_part.size
     return pl.pallas_call(
         ffn_body,
-        out_shape=jax.ShapeDtypeStruct(row_block.shape, jnp.bfloat16),
+        out_shape=[jax.ShapeDtypeStruct(mine.shape, jnp.bfloat16)] * 2,
         grid=(row_total // tile,),
-        in_specs=[rows(), whole(gate_part), whole(up_part), whole(down_part)],
-        out_specs=rows(),
-        compiler_params=pltpu.CompilerParams(vmem_limit_bytes=40 << 20),
+        in_specs=[rows(), rows(), whole(gate_part), whole(up_part), whole(down_part)],
+        out_specs=[rows(), rows()],
+        compiler_params=pltpu.CompilerParams(vmem_limit_bytes=48 << 20),
         cost_estimate=pl.CostEstimate(
-            flops=2 * row_total * weight_count,
-            bytes_accessed=2 * weight_count + 4 * row_total * feature_count,
-            transcendentals=row_total * gate_part.shape[2],
+            flops=4 * row_total * weight_count,
+            bytes_accessed=2 * weight_count + 8 * row_total * feature_count,
+            transcendentals=2 * row_total * gate_part.shape[1],
         ),
-    )(row_block, gate_part, up_part, down_part)
+    )(mine, theirs, gate_part, up_part, down_part)
+
+
+def pack_body(hot_ref, row_ref, out_ref):
+    out_ref[...] = jnp.dot(hot_ref[...], row_ref[...], preferred_element_type=jnp.float32).astype(
+        out_ref.dtype
+    )
+
+
+def pack_rows(hot, rows):
+    slot_total, row_count = hot.shape
+    feature_count = rows.shape[1]
+    tile = 256
+    return pl.pallas_call(
+        pack_body,
+        out_shape=jax.ShapeDtypeStruct((slot_total, feature_count), jnp.bfloat16),
+        grid=(slot_total // tile,),
+        in_specs=[
+            pl.BlockSpec((tile, row_count), lambda i: (i, 0)),
+            pl.BlockSpec((row_count, feature_count), lambda i: (0, 0)),
+        ],
+        out_specs=pl.BlockSpec((tile, feature_count), lambda i: (i, 0)),
+        cost_estimate=pl.CostEstimate(
+            flops=2 * slot_total * row_count * feature_count,
+            bytes_accessed=2 * slot_total * feature_count,
+            transcendentals=0,
+        ),
+    )(hot, rows)
 
 
 def attend(query_block, key_block, value_block, sink_logits, query_pos, key_pos):
@@ -144,26 +179,39 @@
         * norm_gain
     )
     rotated = rotate_rows(normed)
-    packed = jnp.dot(
-        slot_hot.astype(jnp.bfloat16).T, rotated, preferred_element_type=jnp.float32
-    ).astype(jnp.bfloat16)
     expert_total = lax.axis_size(CHIPS)
-    outgoing = packed.reshape(expert_total, -1, feature_count)
-    arrived = lax.all_to_all(outgoing, CHIPS, split_axis=0, concat_axis=0, tiled=True)
-    mine = arrived.reshape(-1, feature_count)
-    swap = [(0, 1), (1, 0)]
-    theirs = lax.ppermute(mine, "core", swap)
-    made_mine = expert_half(mine, gate_weight, up_weight, down_weight)
-    made_theirs = expert_half(theirs, gate_weight, up_weight, down_weight)
-    other_half = lax.ppermute(made_theirs, "core", swap)
-    summed = (made_mine.astype(jnp.float32) + other_half.astype(jnp.float32)).astype(jnp.bfloat16)
-    returned = lax.all_to_all(
-        summed.reshape(arrived.shape), CHIPS, split_axis=0, concat_axis=0, tiled=True
-    ).reshape(-1, feature_count)
+    slot_total = slot_hot.shape[1]
+    step = slot_total // CHUNKS
+    hot_rows = slot_hot.astype(jnp.bfloat16).T
     gate_high = lax.reduce_precision(slot_gate, 8, 7)
     gate_parts = jnp.concatenate([gate_high, slot_gate - gate_high], axis=0).astype(jnp.bfloat16)
-    weighted = jnp.dot(gate_parts, returned, preferred_element_type=jnp.float32)
-    expert_sum = weighted[:row_count] + weighted[row_count:]
+    gate_turned = jnp.swapaxes(gate_weight, 1, 2)
+    up_turned = jnp.swapaxes(up_weight, 1, 2)
+    swap = [(0, 1), (1, 0)]
+
+    def exchange(blocks):
+        return lax.all_to_all(blocks, CHIPS, split_axis=0, concat_axis=0, tiled=True)
+
+    expert_sum = 0.0
+    for chunk in range(CHUNKS):
+        part = slice(chunk * step, (chunk + 1) * step)
+        outgoing = pack_rows(hot_rows[part], rotated).reshape(expert_total, -1, feature_count)
+        arrived = exchange(outgoing)
+        theirs = lax.ppermute(arrived, "core", swap)
+        made_mine, made_theirs = expert_half(
+            arrived.reshape(step, feature_count),
+            theirs.reshape(step, feature_count),
+            gate_turned,
+            up_turned,
+            down_weight,
+        )
+        other_half = lax.ppermute(made_theirs.reshape(arrived.shape), "core", swap)
+        summed = made_mine.reshape(arrived.shape).astype(jnp.float32) + other_half.astype(
+            jnp.float32
+        )
+        returned = exchange(summed.astype(jnp.bfloat16)).reshape(step, feature_count)
+        weighted = jnp.dot(gate_parts[:, part], returned, preferred_element_type=jnp.float32)
+        expert_sum = expert_sum + weighted[:row_count] + weighted[row_count:]
     return (mid_stream + expert_sum).astype(jnp.bfloat16)
 
 
@@ -177,7 +225,10 @@
     earlier = (row_axis[:, None] > row_axis[None, :]).astype(jnp.float32)
     rank = jnp.dot(earlier, chosen, preferred_element_type=jnp.float32)
     route_rank = jnp.sum(jnp.where(named, rank[:, None, :], 0.0), axis=2).astype(jnp.int32)
-    slot = expert_ids * capacity + route_rank
+    depth = capacity // CHUNKS
+    slot = (
+        route_rank // depth * (expert_total * depth) + expert_ids * depth + route_rank % depth
+    )
     slots = jnp.arange(expert_total * capacity, dtype=jnp.int32)
     slot_hot = jnp.zeros((row_count, slots.shape[0]), jnp.float32)
     slot_gate = slot_hot

time: 435 us -> 341 us (0.78)
  local copies, waits for them, and re-layouts: 73.3 us -> 6.07 us
  blocking collectives: 137 us -> 72.8 us
  waiting for transfers between devices: 137 us -> 158 us
  Pallas kernels: 35.8 us -> 49.9 us
  starting transfers between devices: 13.2 us -> 22.5 us
    all_to_all x1, blocking collectives: 137 us -> 72.8 us  [exchange(): lax.all_to_all(blocks, CHIPS, split_axis=0, concat_axis=0, tiled=True)]
    unnamed x25 -> x19, local copies, waits for them, and re-layouts: 30 us -> 3.22 us
    ppermute x2 -> x0, local copies, waits for them, and re-layouts: 17 us -> none  [the longest x1 8.5 us: local(): other_half = lax.ppermute(made_theirs, 'core', swap)]
    all_to_all x1 -> x3, waiting for transfers between devices: 137 us -> 152 us  [exchange(): lax.all_to_all(blocks, CHIPS, split_axis=0, concat_axis=0, tiled=True)]
    pallas_call x2 -> x4, Pallas kernels: 35.8 us -> 49.9 us  [the longest x2 42.4 us: expert_half(): pl.pallas_call(ffn_body, out_shape=[jax.ShapeDtypeStruct(mine.shape, jnp....]
    all_to_all x1 -> x3, starting transfers between devices: 7.28 us -> 17 us  [exchange(): lax.all_to_all(blocks, CHIPS, split_axis=0, concat_axis=0, tiled=True)]
    reshape x1 -> x0, local copies, waits for them, and re-layouts: 8.45 us -> none  [local(): mine = arrived.reshape(-1, feature_count)]
    pallas_call x1 -> x0, local copies, waits for them, and re-layouts: 8.44 us -> none  [expert_half(): pl.pallas_call(ffn_body, out_shape=jax.ShapeDtypeStruct(row_block.shape,...]
  transfers between devices with their start and end apart: 5 -> 9, of which waited for: 1 -> 4; matrix products, arithmetic and copies ran while one was open for 5% -> 5% of each run, Pallas kernels for 4% -> 14%
where the time goes in v2:
time: 341 us; the launch traced here: 340 us
  waiting for transfers between devices  158 us (46%)
  blocking collectives  72.8 us (21%)
  Pallas kernels  49.9 us (15%)
  starting transfers between devices  22.5 us (7%)
  matrix products  18.1 us (5%)
  other arithmetic  12.9 us (4%)
  local copies, waits for them, and re-layouts  6.07 us (2%)
    all_to_all x3, waiting for transfers between devices, exchange(): lax.all_to_all(blocks, CHIPS, split_axis=0, concat_axis=0, tiled=True)  152 us
    all_to_all x1, blocking collectives, exchange(): lax.all_to_all(blocks, CHIPS, split_axis=0, concat_axis=0, tiled=True)  72.8 us
    pallas_call x2, Pallas kernels, expert_half(): pl.pallas_call(ffn_body, out_shape=[jax.ShapeDtypeStruct(mine.shape, jnp....  42.4 us
    all_to_all x3, starting transfers between devices, exchange(): lax.all_to_all(blocks, CHIPS, split_axis=0, concat_axis=0, tiled=True)  17 us
    pallas_call x2, Pallas kernels, pack_rows(): pl.pallas_call(pack_body, out_shape=jax.ShapeDtypeStruct((slot_total, fea...  7.48 us
  transfers between devices with their start and end apart: 9, of which 4 were waited for; matrix products, arithmetic and copies ran while one was open for 5% of the time, Pallas kernels for 14%

profile of v2, /device:TPU:14, one launch (start us, length us, event | category | flops | bytes accessed | tf_op | source)
XLA Modules:
  0.0 340.3 jit_solution(16460364282823546858)
XLA Ops:
  0.0 1.9 collective-permute-start.1
  1.9 3.5 %collective-permute-start = (bf16[128,256]{1,0:T(8,128)(2,1)}, bf16[128,256]{1,0:T(8,128)(2,1)S(1)}, u32[]{:S(2)}, u32[]{:S(2)}) collective-permute-start(bf16[128,256]{1,0:T(8,128)(2,1)} %param.15), channel_id=1, source_target_pairs={{0,1},{1,2},{2,3},{3,4},{4,5},{5,6},{6,7},{7,8},{8,9},{9,10},{10,1... | collective-permute-start | bytes 196616 | tf_op jit(solution)/shard_map/ppermute | solution.py:24
  5.5 1.3 copy.30
  6.8 0.7 max.17
  8.4 0.7 select_reduce_fusion
  9.1 0.7 fusion.46
  10.0 0.7 fusion.65
  10.9 0.9 pad_maximum_fusion.3
  11.8 0.8 fusion.3
  12.7 1.9 copy-done
  14.6 0.9 fusion.2
  15.7 3.4 %fusion.7 = bf16[4,64,8,128]{3,1,2,0:T(8,128)(2,1)S(1)} fusion(bf16[256,4,64,1]{0,2,3,1:T(8,128)(2,1)S(1)} %bitcast.82, f32[4,256,128,8]{2,1,3,0:T(8,128)} %copy-done, f32[4,8,128]{2,1,0:T(8,128)S(1)} %exponential_add_fusion, f32[4,8,128]{2,1,0:T(8,128)S(1)} %broadcast_maximum_fusion, pred[128,256]{0,1:T(8,128)(4,1)S(1)} %and_and_fusion), kind=kOutput, calls=%fused_computation.19 | convolution fusion | flops 139722752 | bytes 4915200 | tf_op jit(solution)/shard_map/kgts,skd->tkgd/dot_general | solution.py:129
  19.2 6.1 %multiply_reduce_fusion = (f32[128]{0:T(128)S(1)}, f32[128,2880]{0,1:T(8,128)S(1)}) fusion(bf16[2048,2880]{0,1:T(8,128)(2,1)} %param.17, bf16[128,2048]{0,1:T(8,128)(2,1)S(1)} %bitcast.87, bf16[128,2880]{0,1:T(8,128)(2,1)S(1)} %copy-done.8), kind=kOutput, calls=%fused_computation.17 | convolution fusion | flops 1511423872 | bytes 14533120 | tf_op jit(solution)/shard_map/dot_general | solution.py:173
  25.8 1.4 convolution_convert_fusion
  27.3 1.2 copy.32.row_ref
  28.5 3.4 %shard_map.118 = bf16[512,2880]{1,0:T(8,128)(2,1)} custom-call(bf16[512,128]{1,0:T(8,128)(2,1)} %get-tuple-element.13.hot_ref, bf16[128,2880]{1,0:T(8,128)(2,1)} %copy.32.row_ref), custom_call_target="tpu_custom_call" | custom-call | flops 377487360 | bytes 2949120 | tf_op jit(solution)/shard_map/pallas_call | solution.py:96
  31.9 72.8 %all_to_all.20 = bf16[16,32,2880]{2,1,0:T(8,128)(2,1)S(1)} all-to-all(bf16[16,32,2880]{2,1,0:T(8,128)(2,1)} %bitcast.76), channel_id=1, replica_groups=mesh['ctx'=4,'chip'=4,'core'=2] {'ctx','chip'}, dimensions={0} | all-to-all | bytes 5898240 | tf_op jit(solution)/shard_map/all_to_all | solution.py:193
  104.7 4.1 %shard_map.120 = bf16[512,2880]{1,0:T(8,128)(2,1)} custom-call(bf16[512,128]{1,0:T(8,128)(2,1)} %get-tuple-element.14.hot_ref, bf16[128,2880]{1,0:T(8,128)(2,1)} %copy.32.row_ref), custom_call_target="tpu_custom_call" | custom-call | flops 377487360 | bytes 2949120 | tf_op jit(solution)/shard_map/pallas_call | solution.py:96
  108.7 6.7 %all-to-all-start.2 = ((bf16[16,32,2880]{2,1,0:T(8,128)(2,1)}), bf16[16,32,2880]{2,1,0:T(8,128)(2,1)}, u32[]{:S(2)}, u32[]{:S(2)}) async-start(bf16[16,32,2880]{2,1,0:T(8,128)(2,1)} %bitcast.75), calls=%async_computation.2 | async-start | bytes 6029312 | tf_op jit(solution)/shard_map/all_to_all | solution.py:193
  115.5 21.8 %shard_map.119 = (bf16[512,2880]{1,0:T(8,128)(2,1)S(1)}, bf16[512,2880]{1,0:T(8,128)(2,1)}) custom-call(bf16[512,2880]{1,0:T(8,128)(2,1)} %bitcast.78, bf16[512,2880]{1,0:T(8,128)(2,1)} %bitcast.23.theirs_ref, bf16[1,720,2880]{2,1,0:T(8,128)(2,1)} %bitcast.83, bf16[1,720,2880]{2,1,0:T(8,128)(2,1)} %bitcast.85, bf16[1,720,2880]{2,1,0:T(8,128)(2,1)} %down_ref.3), custom_call_target="tpu_custom_call" | custom-call | flops 12740198400 | bytes 24238080 | tf_op jit(solution)/shard_map/pallas_call | solution.py:71
  137.2 47.0 %all-to-all-done.2 = bf16[16,32,2880]{2,1,0:T(8,128)(2,1)} async-done(((bf16[16,32,2880]{2,1,0:T(8,128)(2,1)}), bf16[16,32,2880]{2,1,0:T(8,128)(2,1)}, u32[]{:S(2)}, u32[]{:S(2)}) %all-to-all-start.2) | async-done | bytes 2949152 | tf_op jit(solution)/shard_map/all_to_all | solution.py:193
  184.2 4.1 %fusion.1 = bf16[16,32,2880]{2,1,0:T(8,128)(2,1)} fusion(bf16[16,32,2880]{2,1,0:T(8,128)(2,1)S(1)} %bitcast.71, bf16[16,32,2880]{2,1,0:T(8,128)(2,1)} %collective-permute-done.3), kind=kLoop, calls=%fused_computation.3 | loop fusion | flops 5898240 | bytes 8847360 | tf_op jit(solution)/shard_map/convert_element_type | solution.py:212
  188.4 5.1 %all-to-all-start.1 = ((bf16[16,32,2880]{2,1,0:T(8,128)(2,1)}), bf16[16,32,2880]{2,1,0:T(8,128)(2,1)S(1)}, u32[]{:S(2)}, u32[]{:S(2)}) async-start(bf16[16,32,2880]{2,1,0:T(8,128)(2,1)} %fusion.1), calls=%async_computation.1 | async-start | bytes 6029312 | tf_op jit(solution)/shard_map/all_to_all | solution.py:193
  193.5 20.6 %shard_map.121 = (bf16[512,2880]{1,0:T(8,128)(2,1)S(1)}, bf16[512,2880]{1,0:T(8,128)(2,1)S(1)}) custom-call(bf16[512,2880]{1,0:T(8,128)(2,1)} %bitcast.30.mine_ref, bf16[512,2880]{1,0:T(8,128)(2,1)} %bitcast.31.theirs_ref, bf16[1,720,2880]{2,1,0:T(8,128)(2,1)} %bitcast.84, bf16[1,720,2880]{2,1,0:T(8,128)(2,1)} %bitcast.86, bf16[1,720,2880]{2,1,0:T(8,128)(2,1)} %down_ref.3), custom_call_target="tpu_custom_call" | custom-call | flops 12740198400 | bytes 24238080 | tf_op jit(solution)/shard_map/pallas_call | solution.py:71
  214.2 5.5 %collective-permute-done.5 = bf16[16,32,2880]{2,1,0:T(8,128)(2,1)S(1)} collective-permute-done((bf16[16,32,2880]{2,1,0:T(8,128)(2,1)S(1)}, bf16[16,32,2880]{2,1,0:T(8,128)(2,1)S(1)}, u32[]{:S(2)}, u32[]{:S(2)}) %collective-permute-start.5) | collective-permute-done | bytes 2949152 | tf_op jit(solution)/shard_map/ppermute | solution.py:208
  219.7 2.3 fusion
  222.0 41.5 %all-to-all-done.1 = bf16[16,32,2880]{2,1,0:T(8,128)(2,1)S(1)} async-done(((bf16[16,32,2880]{2,1,0:T(8,128)(2,1)}), bf16[16,32,2880]{2,1,0:T(8,128)(2,1)S(1)}, u32[]{:S(2)}, u32[]{:S(2)}) %all-to-all-start.1) | async-done | bytes 2949152 | tf_op jit(solution)/shard_map/all_to_all | solution.py:193
  263.5 5.1 %all-to-all-start.3 = ((bf16[16,32,2880]{2,1,0:T(8,128)(2,1)}), bf16[16,32,2880]{2,1,0:T(8,128)(2,1)}, u32[]{:S(2)}, u32[]{:S(2)}) async-start(bf16[16,32,2880]{2,1,0:T(8,128)(2,1)} %fusion), calls=%async_computation.3 | async-start | bytes 6029312 | tf_op jit(solution)/shard_map/all_to_all | solution.py:193
  269.1 2.9 fusion.10
  272.0 63.9 %all-to-all-done.3 = bf16[16,32,2880]{2,1,0:T(8,128)(2,1)} async-done(((bf16[16,32,2880]{2,1,0:T(8,128)(2,1)}), bf16[16,32,2880]{2,1,0:T(8,128)(2,1)}, u32[]{:S(2)}, u32[]{:S(2)}) %all-to-all-start.3) | async-done | bytes 2949152 | tf_op jit(solution)/shard_map/all_to_all | solution.py:193
  335.8 3.3 fusion.12
  339.2 1.2 fusion.6
  (46 shorter events, 2.5 us)
Async XLA Ops:
  0.0 10.9 %collective-permute-start.1 = (bf16[128,256]{1,0:T(8,128)(2,1)}, bf16[128,256]{1,0:T(8,128)(2,1)S(1)}, u32[]{:S(2)}, u32[]{:S(2)}) collective-permute-start(bf16[128,256]{1,0:T(8,128)(2,1)} %param.14), channel_id=1, source_target_pairs={{0,1},{1,2},{2,3},{3,4},{4,5},{5,6},{6,7},{7,8},{8,9},{9,10},{10,1... | collective-permute-start | bytes 196616 | tf_op jit(solution)/shard_map/ppermute | solution.py:24
  1.9 13.7 %collective-permute-start = (bf16[128,256]{1,0:T(8,128)(2,1)}, bf16[128,256]{1,0:T(8,128)(2,1)S(1)}, u32[]{:S(2)}, u32[]{:S(2)}) collective-permute-start(bf16[128,256]{1,0:T(8,128)(2,1)} %param.15), channel_id=1, source_target_pairs={{0,1},{1,2},{2,3},{3,4},{4,5},{5,6},{6,7},{7,8},{8,9},{9,10},{10,1... | collective-permute-start | bytes 196616 | tf_op jit(solution)/shard_map/ppermute | solution.py:24
  12.6 2.0 copy-start
  12.6 3.0 copy-start.5
  15.7 3.4 %copy-start.8 = (bf16[128,2880]{0,1:T(8,128)(2,1)S(1)}, bf16[128,2880]{0,1:T(8,128)(2,1)}, u32[]{:S(2)}) copy-start(bf16[128,2880]{0,1:T(8,128)(2,1)} %param.12) | copy-start | bytes 2211844
  19.2 6.2 %copy-start.6 = (f32[2880]{0:T(1024)S(1)}, f32[2880]{0:T(1024)}, u32[]{:S(2)}) copy-start(f32[2880]{0:T(1024)} %param.18) | copy-start | bytes 34564
  25.3 1.9 copy-start.2
  104.7 4.1 %copy-start.4 = (bf16[16,32,2880]{2,1,0:T(8,128)(2,1)}, bf16[16,32,2880]{2,1,0:T(8,128)(2,1)S(1)}, u32[]{:S(2)}) copy-start(bf16[16,32,2880]{2,1,0:T(8,128)(2,1)S(1)} %all_to_all.20) | copy-start | bytes 8847364
  104.7 10.8 %collective-permute-start.2 = (bf16[16,32,2880]{2,1,0:T(8,128)(2,1)S(1)}, bf16[16,32,2880]{2,1,0:T(8,128)(2,1)}, u32[]{:S(2)}, u32[]{:S(2)}) collective-permute-start(bf16[16,32,2880]{2,1,0:T(8,128)(2,1)S(1)} %all_to_all.20), channel_id=1, source_target_pairs={{0,1},{1,0},{2,3},{3,2},{4,5},{5,4},{6,7},{7,6},{8,9},{9,8},{10,11... | collective-permute-start | bytes 8847368 | tf_op jit(solution)/shard_map/ppermute | solution.py:200
  108.7 75.5 %all-to-all-start.2 = ((bf16[16,32,2880]{2,1,0:T(8,128)(2,1)}), bf16[16,32,2880]{2,1,0:T(8,128)(2,1)}, u32[]{:S(2)}, u32[]{:S(2)}) async-start(bf16[16,32,2880]{2,1,0:T(8,128)(2,1)} %bitcast.75), calls=%async_computation.2 | async-start | bytes 6029312 | tf_op jit(solution)/shard_map/all_to_all | solution.py:193
  137.2 47.0 %collective-permute-start.3 = (bf16[16,32,2880]{2,1,0:T(8,128)(2,1)}, bf16[16,32,2880]{2,1,0:T(8,128)(2,1)}, u32[]{:S(2)}, u32[]{:S(2)}) collective-permute-start(bf16[16,32,2880]{2,1,0:T(8,128)(2,1)} %bitcast.27), channel_id=1, source_target_pairs={{0,1},{1,0},{2,3},{3,2},{4,5},{5,4},{6,7},{7,6},{8,9},{9,8},{10,11... | collective-permute-start | bytes 8847368 | tf_op jit(solution)/shard_map/ppermute | solution.py:208
  184.2 9.3 %collective-permute-start.4 = (bf16[16,32,2880]{2,1,0:T(8,128)(2,1)}, bf16[16,32,2880]{2,1,0:T(8,128)(2,1)}, u32[]{:S(2)}, u32[]{:S(2)}) collective-permute-start(bf16[16,32,2880]{2,1,0:T(8,128)(2,1)} %all-to-all-done.2), channel_id=1, source_target_pairs={{0,1},{1,0},{2,3},{3,2},{4,5},{5,4},{6,7},{7,6},{8,9},{9,8},{10,11... | collective-permute-start | bytes 8847368 | tf_op jit(solution)/shard_map/ppermute | solution.py:200
  188.4 75.1 %all-to-all-start.1 = ((bf16[16,32,2880]{2,1,0:T(8,128)(2,1)}), bf16[16,32,2880]{2,1,0:T(8,128)(2,1)S(1)}, u32[]{:S(2)}, u32[]{:S(2)}) async-start(bf16[16,32,2880]{2,1,0:T(8,128)(2,1)} %fusion.1), calls=%async_computation.1 | async-start | bytes 6029312 | tf_op jit(solution)/shard_map/all_to_all | solution.py:193
  214.1 5.5 %collective-permute-start.5 = (bf16[16,32,2880]{2,1,0:T(8,128)(2,1)S(1)}, bf16[16,32,2880]{2,1,0:T(8,128)(2,1)S(1)}, u32[]{:S(2)}, u32[]{:S(2)}) collective-permute-start(bf16[16,32,2880]{2,1,0:T(8,128)(2,1)S(1)} %bitcast.73), channel_id=1, source_target_pairs={{0,1},{1,0},{2,3},{3,2},{4,5},{5,4},{6,7},{7,6},{8,9},{9,8},{10,11... | collective-permute-start | bytes 8847368 | tf_op jit(solution)/shard_map/ppermute | solution.py:208
  222.0 46.6 %copy-start.7 = (f32[128,4]{0,1:T(4,128)S(1)}, f32[128,4]{0,1:T(4,128)}, u32[]{:S(2)}) copy-start(f32[128,4]{0,1:T(4,128)} %param.23) | copy-start | bytes 6148
  263.5 72.3 %all-to-all-start.3 = ((bf16[16,32,2880]{2,1,0:T(8,128)(2,1)}), bf16[16,32,2880]{2,1,0:T(8,128)(2,1)}, u32[]{:S(2)}, u32[]{:S(2)}) async-start(bf16[16,32,2880]{2,1,0:T(8,128)(2,1)} %fusion), calls=%async_computation.3 | async-start | bytes 6029312 | tf_op jit(solution)/shard_map/all_to_all | solution.py:193
  335.8 3.3 copy-start.1
  335.8 3.3 copy-start.3
